TPU v7x, 256 devices: a whole 4x4x8 slice. The times are simulated.
256 devices in a mesh: row: 32 (over z_lo, y, x), col: 8 (over z_hi, core).
Axes of the slice: x: 4, y: 4, z: 8 (z_hi: 4, z_lo: 2; z = z_hi * 2 + z_lo), core: 2. Of those that a mesh axis runs over, the one named last changes fastest.
Arguments:
- c_left: float32 [32, 8, 2048, 256], P('row', 'col'), may hold values from -6 to 6
- c_right: float32 [32, 8, 2048, 256], P('row', 'col'), may hold values from -6 to 6
- c_rank: int32 [32, 8], P('row', 'col'), may hold values from 32 to 256, as said below
- a_left: bfloat16 [32, 2, 2048, 256], P('row', None, 'col'), may hold values from -6 to 6
- a_right: bfloat16 [32, 2, 2048, 256], P('row', None, 'col'), may hold values from -0.125 to 0.125
- a_rank: int32 [32, 2], P('row'), may hold values from 32 to 256, as said below
- a_pattern: int32 [32, 2], P('row'), may hold values 0 or 1
- b_left: bfloat16 [2, 8, 2048, 256], P(None, 'col', 'row'), may hold values from -6 to 6
- b_right: bfloat16 [2, 8, 2048, 256], P(None, 'col', 'row'), may hold values from -0.375 to 0.375
- b_rank: int32 [2, 8], P(None, 'col'), may hold values from 32 to 256, as said below
- b_pattern: int32 [2, 8], P(None, 'col'), may hold values 0 or 1
- probe: bfloat16 [2, 2048, 256], replicated, may hold values from -6 to 6
- target: int32 [32, 8, 2], P('row', 'col'), may hold values from 16 to 240, as said below
Outputs:
- out_left: float32 [32, 8, 2048, 256], P('row', 'col')
- out_right: float32 [32, 8, 2048, 256], P('row', 'col')
Inputs may be any that keep to these rules, and one draw needn't show every extreme that they name: `c_rank`: every rank lies from 32 to 256; both ends are taken by some tile. `a_rank`: every rank lies from 32 to 256; both ends are taken by some tile. `b_rank`: every rank lies from 32 to 256; both ends are taken by some tile. With g(r) = max(8, r // 16): target[i, j, 0] <= c_rank[i, j] - g(c_rank[i, j]) and target[i, j, k] <= target[i, j, k - 1] - g(target[i, j, k - 1]); both ends are taken by some tile.
All inputs are finite; a program needn't handle non-finite values. No bound on the sum of `a_pattern` or of `b_pattern` on one device may be relied on, other than what follows from the above.
Results may differ from a plain program's by a relative error of at most 0.0009.
Values may be sent and summed in bfloat16 or wider, within the bound.
A program may use at most 128 MiB of HBM per device.

v0:
```python
import math

import jax
import jax.numpy as jnp
from jax import lax
from jax.sharding import PartitionSpec as P


def column_mask(count, width):
    return (jnp.arange(width, dtype=jnp.int32) < count).astype(jnp.float32)


def product_of(left, right):
    return jnp.dot(left, right, precision=lax.Precision.HIGHEST, preferred_element_type=jnp.float32)


def transposed_product(left, right):
    return lax.dot_general(
        left,
        right,
        (((0,), (0,)), ((), ())),
        precision=lax.Precision.HIGHEST,
        preferred_element_type=jnp.float32,
    )


def recompress(left, right, keep, extra, extra_right, right_probe, probe_step, tmask):
    tile = left.shape[0]
    probe_cols = probe_step.astype(jnp.float32) * tmask[None, :]
    core_c = transposed_product(right, probe_cols) * keep[:, None]
    core_b = right_probe * tmask[None, :]
    sample = product_of(left, core_c) + product_of(extra, core_b)
    gram = transposed_product(sample, sample) + jnp.diag(1.0 - tmask)
    factor = jnp.linalg.cholesky(gram)
    basis = lax.linalg.triangular_solve(
        factor, sample, left_side=False, lower=True, transpose_a=True
    )
    back_c = transposed_product(left, basis) * keep[:, None]
    back_b = transposed_product(extra, basis)
    new_right = (product_of(right, back_c) + product_of(extra_right, back_b)) / math.sqrt(tile)
    return (basis * math.sqrt(tile), new_right)


def on_device(
    c_left,
    c_right,
    c_rank,
    a_left,
    a_right,
    a_rank,
    a_pattern,
    b_left,
    b_right,
    b_rank,
    b_pattern,
    probe,
    target,
):
    width = c_left.shape[3]
    steps = probe.shape[0]
    left = c_left[0, 0]
    right = c_right[0, 0]
    keep = column_mask(c_rank[0, 0], width)
    for step in range(steps):
        a_l, a_r = (
            lax.all_gather(a_left[0, step], "col", axis=0, tiled=True),
            lax.all_gather(a_right[0, step], "col", axis=0, tiled=True),
        )
        b_r = lax.all_gather(b_right[step, 0], "row", axis=0, tiled=True)

        def add_middle(total, piece, start, a_rows=a_r):
            return lax.dot_general(
                a_rows, piece, (((0,), (0,)), ((), ())), preferred_element_type=jnp.float32
            )

        middle = add_middle(
            jnp.zeros((width, width), jnp.float32),
            lax.all_gather(b_left[step, 0], "row", axis=0, tiled=True),
            jnp.int32(0),
        )
        weight = (a_pattern[0, step] * b_pattern[step, 0]).astype(jnp.float32)
        middle = (
            middle
            * column_mask(a_rank[0, step], width)[:, None]
            * column_mask(b_rank[step, 0], width)[None, :]
            * weight
        )
        extra = product_of(a_l.astype(jnp.float32), middle)
        right_probe = lax.dot_general(
            b_r, probe[step], (((0,), (0,)), ((), ())), preferred_element_type=jnp.float32
        )
        tmask = column_mask(target[0, 0, step], width)
        left, right = recompress(
            left, right, keep, extra, b_r.astype(jnp.float32), right_probe, probe[step], tmask
        )
        keep = tmask
    return (left[None, None], right[None, None])


def solution(mesh):
    return jax.shard_map(
        on_device,
        mesh=mesh,
        in_specs=(
            P("row", "col", None, None),
            P("row", "col", None, None),
            P("row", "col"),
            P("row", None, "col", None),
            P("row", None, "col", None),
            P("row", None),
            P("row", None),
            P(None, "col", "row", None),
            P(None, "col", "row", None),
            P(None, "col"),
            P(None, "col"),
            P(),
            P("row", "col", None),
        ),
        out_specs=(P("row", "col", None, None), P("row", "col", None, None)),
        check_vma=False,
    )
```

profile of v0, /device:TPU:1, one launch (start us, length us, event | category | flops | bytes accessed | tf_op | source)
XLA Modules:
  0.0 865.4 jit_solution(7371660439607618762)
XLA Ops:
  7.2 1.5 fusion.94
  8.8 1.7 fusion.93
  10.6 1.4 fusion.95
  12.1 1.7 fusion.92
  31.7 5.4 fusion.23
  37.1 3.3 convolution_bitcast_fusion.1
  40.4 104.2 %all-gather.23.cloned.1.call-done = bf16[1,1,2048,256]{3,2,1,0:T(8,128)(2,1)} async-done(((bf16[1,1,64,256]{3,2,1,0:T(8,128)(2,1)}), bf16[1,1,2048,256]{3,2,1,0:T(8,128)(2,1)}) %all-gather.23.cloned.1.call-update) | async-done | bytes 1048592 | tf_op jit(solution)/shard_map/all_gather | solution.py:69
  144.6 2.0 convolution_multiply_fusion.2
  146.6 53.8 %all-gather.17.cloned.1.call-done = bf16[1,1,2048,256]{3,2,1,0:T(8,128)(2,1)} async-done(((bf16[1,1,256,256]{3,2,1,0:T(8,128)(2,1)}), bf16[1,1,2048,256]{3,2,1,0:T(8,128)(2,1)}) %all-gather.17.cloned.1.call-update) | async-done | bytes 1048592 | tf_op jit(solution)/shard_map/all_gather | solution.py:67
  200.4 130.3 %all-gather.19.cloned.1.call-done = bf16[1,1,2048,256]{3,2,1,0:T(8,128)(2,1)} async-done(((bf16[1,1,64,256]{3,2,1,0:T(8,128)(2,1)}), bf16[1,1,2048,256]{3,2,1,0:T(8,128)(2,1)}) %all-gather.19.cloned.1.call-update) | async-done | bytes 1048592 | tf_op jit(solution)/shard_map/all_gather | solution.py:78
  330.7 2.0 fusion.37
  332.7 53.1 %all-gather.21.cloned.1.call-done = bf16[1,1,2048,256]{3,2,1,0:T(8,128)(2,1)} async-done(((bf16[1,1,256,256]{3,2,1,0:T(8,128)(2,1)}), bf16[1,1,2048,256]{3,2,1,0:T(8,128)(2,1)}) %all-gather.21.cloned.1.call-update) | async-done | bytes 1048592 | tf_op jit(solution)/shard_map/all_gather | solution.py:66
  385.8 3.2 fusion.54
  389.1 2.1 convolution_add_fusion.3
  392.5 2.1 convolution_add_fusion.5
  394.8 11.7 %cholesky.130 = f32[128,128]{1,0:T(8,128)S(1)} custom-call(f32[128,128]{1,0:T(8,128)S(1)} %cholesky.194), custom_call_target="Cholesky" | custom-call | tf_op jit(solution)/shard_map/jit(cholesky)/cholesky | solution.py:34
  407.2 9.8 %custom-call.13 = f32[1,128,128]{1,2,0:T(8,128)S(1)} custom-call(f32[1,128,128]{2,1,0:T(8,128)S(1)} %get-tuple-element.57), custom_call_target="InvertDiagBlocksLowerTriangular" | custom-call | tf_op jit(solution)/shard_map/jit(cholesky)/cholesky | solution.py:34
  417.5 11.7 %cholesky.147 = f32[128,128]{1,0:T(8,128)S(1)} custom-call(f32[128,128]{1,0:T(8,128)S(1)} %convolution_subtract_fusion.3), custom_call_target="Cholesky" | custom-call | tf_op jit(solution)/shard_map/jit(cholesky)/cholesky | solution.py:34
  431.3 4.0 while.4
  435.9 20.1 %custom-call.14 = f32[2,128,128]{1,2,0:T(8,128)S(1)} custom-call(f32[2,128,128]{2,1,0:T(8,128)S(1)} %get-tuple-element.18), custom_call_target="InvertDiagBlocksLowerTriangular" | custom-call | tf_op jit(solution)/shard_map/triangular_solve/custom-call.0 | solution.py:35
  456.0 2.4 fusion.40
  460.6 1.9 fusion.62
  462.6 1.9 fusion.51
  464.4 1.9 fusion.31
  466.4 2.1 fusion.2
  469.8 2.2 fusion.20
  472.1 4.8 fusion.17
  476.8 39.2 %all-gather.31.cloned.1.call-done = bf16[1,1,2048,256]{3,2,1,0:T(8,128)(2,1)} async-done(((bf16[1,1,64,256]{3,2,1,0:T(8,128)(2,1)}), bf16[1,1,2048,256]{3,2,1,0:T(8,128)(2,1)}) %all-gather.31.cloned.1.call-update) | async-done | bytes 1048592 | tf_op jit(solution)/shard_map/all_gather | solution.py:69
  516.1 2.0 convolution_multiply_fusion
  518.1 54.1 %all-gather.25.cloned.1.call-done = bf16[1,1,2048,256]{3,2,1,0:T(8,128)(2,1)} async-done(((bf16[1,1,256,256]{3,2,1,0:T(8,128)(2,1)}), bf16[1,1,2048,256]{3,2,1,0:T(8,128)(2,1)}) %all-gather.25.cloned.1.call-update) | async-done | bytes 1048592 | tf_op jit(solution)/shard_map/all_gather | solution.py:67
  572.2 130.3 %all-gather.27.cloned.1.call-done = bf16[1,1,2048,256]{3,2,1,0:T(8,128)(2,1)} async-done(((bf16[1,1,64,256]{3,2,1,0:T(8,128)(2,1)}), bf16[1,1,2048,256]{3,2,1,0:T(8,128)(2,1)}) %all-gather.27.cloned.1.call-update) | async-done | bytes 1048592 | tf_op jit(solution)/shard_map/all_gather | solution.py:78
  702.5 2.7 fusion.35
  705.2 52.5 %all-gather.29.cloned.1.call-done = bf16[1,1,2048,256]{3,2,1,0:T(8,128)(2,1)} async-done(((bf16[1,1,256,256]{3,2,1,0:T(8,128)(2,1)}), bf16[1,1,2048,256]{3,2,1,0:T(8,128)(2,1)}) %all-gather.29.cloned.1.call-update) | async-done | bytes 1048592 | tf_op jit(solution)/shard_map/all_gather | solution.py:66
  757.7 3.3 fusion.44
  761.1 3.6 convolution_add_fusion.1
  766.0 3.8 convolution_add_fusion.4
  772.4 11.7 %cholesky.164 = f32[128,128]{1,0:T(8,128)S(1)} custom-call(f32[128,128]{1,0:T(8,128)S(1)} %cholesky.197), custom_call_target="Cholesky" | custom-call | tf_op jit(solution)/shard_map/jit(cholesky)/cholesky | solution.py:34
  784.8 9.8 %custom-call.15 = f32[1,128,128]{1,2,0:T(8,128)S(1)} custom-call(f32[1,128,128]{2,1,0:T(8,128)S(1)} %get-tuple-element.49), custom_call_target="InvertDiagBlocksLowerTriangular" | custom-call | tf_op jit(solution)/shard_map/jit(cholesky)/cholesky | solution.py:34
  796.8 12.1 %cholesky.181 = f32[128,128]{1,0:T(8,128)S(1)} custom-call(f32[128,128]{1,0:T(8,128)S(1)} %convolution_subtract_fusion.2), custom_call_target="Cholesky" | custom-call | tf_op jit(solution)/shard_map/jit(cholesky)/cholesky | solution.py:34
  812.0 4.0 while.5
  816.7 20.5 %custom-call.16 = f32[2,128,128]{1,2,0:T(8,128)S(1)} custom-call(f32[2,128,128]{2,1,0:T(8,128)} %copy-done.22), custom_call_target="InvertDiagBlocksLowerTriangular" | custom-call | tf_op jit(solution)/shard_map/triangular_solve/custom-call.0 | solution.py:35
  837.2 2.4 fusion.38
  839.6 1.8 convolution_subtract_fusion
  842.6 2.7 fusion.28
  845.2 1.9 fusion.19
  847.1 1.5 multiply_bitcast_fusion
  848.6 3.1 copy.23
  853.4 5.0 fusion.1
  (126 shorter events, 42.3 us)
Async XLA Ops:
  7.2 30.0 %copy-start = (f32[1,1,2048,256]{3,2,1,0:T(8,128)S(1)}, f32[1,1,2048,256]{3,2,1,0:T(8,128)}, u32[]{:S(2)}) copy-start(f32[1,1,2048,256]{3,2,1,0:T(8,128)} %param.16) | copy-start | bytes 6291460
  7.2 137.4 %all-gather.23.cloned.1.call-start = ((), (), s32[]{:S(2)}) async-start(), calls=%async_computation.3 | async-start | bytes 1081344 | tf_op jit(solution)/shard_map/all_gather | solution.py:69
  8.8 191.6 %all-gather.17.cloned.1.call-start = ((), (), s32[]{:S(2)}) async-start(), calls=%async_computation | async-start | bytes 1179648 | tf_op jit(solution)/shard_map/all_gather | solution.py:67
  10.5 320.1 %all-gather.19.cloned.1.call-start = ((), (), s32[]{:S(2)}) async-start(), calls=%async_computation.1 | async-start | bytes 1081344 | tf_op jit(solution)/shard_map/all_gather | solution.py:78
  12.0 373.8 %all-gather.21.cloned.1.call-start = ((), (), s32[]{:S(2)}) async-start(), calls=%async_computation.2 | async-start | bytes 1179648 | tf_op jit(solution)/shard_map/all_gather | solution.py:66
  13.8 502.3 %all-gather.31.cloned.1.call-start = ((), (), s32[]{:S(2)}) async-start(), calls=%async_computation.7 | async-start | bytes 1081344 | tf_op jit(solution)/shard_map/all_gather | solution.py:69
  14.4 557.8 %all-gather.25.cloned.1.call-start = ((), (), s32[]{:S(2)}) async-start(), calls=%async_computation.4 | async-start | bytes 1179648 | tf_op jit(solution)/shard_map/all_gather | solution.py:67
  14.9 687.5 %all-gather.27.cloned.1.call-start = ((), (), s32[]{:S(2)}) async-start(), calls=%async_computation.5 | async-start | bytes 1081344 | tf_op jit(solution)/shard_map/all_gather | solution.py:78
  15.7 742.0 %all-gather.29.cloned.1.call-start = ((), (), s32[]{:S(2)}) async-start(), calls=%async_computation.6 | async-start | bytes 1179648 | tf_op jit(solution)/shard_map/all_gather | solution.py:66
  21.4 19.0 %copy-start.23 = (f32[256]{0:T(256)}, f32[256]{0:T(256)S(1)}, u32[]{:S(2)}) copy-start(f32[256]{0:T(256)S(1)} %compare_convert_fusion.5) | copy-start | bytes 3076
  385.8 3.3 copy-start.15
  389.1 2.1 copy-start.9
  391.2 1.3 copy-start.3
  435.4 0.6 copy-start.26
  456.0 2.4 copy-start.4
  458.4 2.2 copy-start.10
  460.6 11.4 %copy-start.11 = (f32[2048,128]{0,1:T(8,128)}, f32[2048,128]{0,1:T(8,128)S(1)}, u32[]{:S(2)}) copy-start(f32[2048,128]{0,1:T(8,128)S(1)} %fusion.73) | copy-start | bytes 3145732
  460.6 1.9 copy-start.18
  462.6 1.9 copy-start.24
  464.4 1.9 copy-start.13
  466.4 3.5 copy-start.16
  468.5 1.3 copy-start.5
  757.7 3.3 copy-start.14
  761.1 3.6 copy-start.7
  761.1 4.9 copy-start.25
  764.7 1.3 copy-start.1
  769.8 42.2 %copy-start.27 = (s32[2,2]{1,0:T(2,128)S(1)}, s32[2,2]{1,0:T(2,128)}, u32[]{:S(2)}) copy-start(s32[2,2]{1,0:T(2,128)} %copy-done.26) | copy-start | bytes 52
  771.7 0.7 copy-start.20
  808.9 2.1 copy-start.19
  816.0 0.6 copy-start.22
  837.2 2.5 copy-start.2
  839.6 2.9 copy-start.12
  842.6 2.7 copy-start.8
  848.6 3.1 copy-start.17
  851.8 1.6 copy-start.6
  851.8 1.6 copy-start.21
Sparse Core Ops, SparseCore 0:
  9.8 134.7 all-gather.22
  147.0 53.3 all-gather.16
  202.2 128.4 all-gather.18
  332.4 53.3 all-gather.20
  387.4 128.5 all-gather.30
  517.8 54.3 all-gather.24
  574.0 128.4 all-gather.26
  704.3 53.3 all-gather.28
where the time goes:
time: 875 us; the launch traced here: 865 us
  waiting for transfers between devices  620 us (71%)
  other arithmetic  119 us (14%)
  matrix products  73.3 us (8%)
  local copies, waits for them, and re-layouts  31.6 us (4%)
  between operations  20.7 us (2%)
    all_gather x2, waiting for transfers between devices, on_device(): lax.all_gather(b_left[step, 0], 'row', axis=0, tiled=True)  261 us
    all_gather x2, waiting for transfers between devices, on_device(): b_r = lax.all_gather(b_right[step, 0], 'row', axis=0, tiled=True)  143 us
    all_gather x2, waiting for transfers between devices, on_device(): lax.all_gather(a_right[0, step], 'col', axis=0, tiled=True)  108 us
    all_gather x2, waiting for transfers between devices, on_device(): lax.all_gather(a_left[0, step], 'col', axis=0, tiled=True)  106 us
    another operation x14, other arithmetic, recompress(): factor = jnp.linalg.cholesky(gram)  69.7 us
    another operation x5, other arithmetic, recompress(): lax.linalg.triangular_solve(factor, sample, left_side=False, lower=True,...  41.6 us
    dot_general x10, matrix products, product_of(): jnp.dot(left, right, precision=lax.Precision.HIGHEST, preferred_element_t...  30.3 us
    dot_general x8, matrix products, transposed_product(): lax.dot_general(left, right, (((0,), (0,)), ((), ())), precision=lax.Prec...  21.8 us
  transfers between devices with their start and end apart: 8, of which 8 were waited for; matrix products, arithmetic and copies ran while one was open for 14% of the time, Pallas kernels for 0%

commit v1 on v0

v1 whole, which is shorter than its diff:
```python
import functools
import math

import jax
import jax.numpy as jnp
from jax import lax
from jax.experimental import pallas as pl
from jax.experimental.pallas import tpu as pltpu
from jax.sharding import PartitionSpec as P

F32 = jnp.float32
BF16 = jnp.bfloat16
PANEL = 32
CHUNK = 256


def split2(x):
    hi = x.astype(BF16)
    return hi, (x - hi.astype(F32)).astype(BF16)


def split3(x):
    hi = x.astype(BF16)
    rest = x - hi.astype(F32)
    mid = rest.astype(BF16)
    return hi, mid, (rest - mid.astype(F32)).astype(BF16)


def mm(a, b):
    return jnp.dot(a, b, preferred_element_type=F32)


def tmm(a, b):
    return lax.dot_general(a, b, (((0,), (0,)), ((), ())), preferred_element_type=F32)


def mmt(a, b):
    return lax.dot_general(a, b, (((1,), (1,)), ((), ())), preferred_element_type=F32)


def times(op, a, b):
    ah, al = split2(a)
    bh, bl = split2(b)
    return op(ah, bh) + (op(ah, bl) + op(al, bh))


def fine(op, a, b):
    a0, a1, a2 = split3(a)
    b0, b1, b2 = split3(b)
    return op(a0, b0) + ((op(a0, b1) + op(a1, b0)) + (op(a1, b1) + (op(a0, b2) + op(a2, b0))))


def lane(x, c):
    return jnp.broadcast_to(x[:, c : c + 1], (8, 128))


def sublane(x, r):
    return jnp.broadcast_to(x[r : r + 1, :], (8, 128))


def panel_step(p, work, inv_ref):
    width = work.shape[1] // 2
    vregs = work.shape[1] // 128
    groups = PANEL // 8
    rows = [
        [work[8 * g : 8 * g + 8, 128 * v : 128 * v + 128] for v in range(vregs)] for g in range(groups)
    ]
    below = pltpu.roll(work[PANEL:width, :width], width - PANEL, 1)
    sub = lax.broadcasted_iota(jnp.int32, (8, 128), 0)
    for b in range(groups):
        cols = [[lane(rows[g][0], 8 * b + m) for m in range(8)] for g in range(groups)]
        d = [[sublane(cols[b][n], m) for n in range(m + 1)] for m in range(8)]
        heads = [[sublane(rows[b][v], n) for v in range(vregs)] for n in range(8)]
        w = [[None] * 8 for _ in range(8)]
        low = [[None] * 8 for _ in range(8)]
        for k in range(8):
            r = lax.rsqrt(d[k][k])
            w[k][k] = r
            for m in range(k + 1, 8):
                low[m][k] = d[m][k] * r
            for m in range(k + 1, 8):
                for n in range(k + 1, m + 1):
                    d[m][n] = d[m][n] - low[m][k] * low[n][k]
            for n in range(k):
                total = low[k][n] * w[n][n]
                for l in range(n + 1, k):
                    total = total + low[k][l] * w[l][n]
                w[k][n] = -(total * r)
        for v in range(vregs):
            total = None
            for n in range(8):
                column = jnp.zeros((8, 128), F32)
                for m in range(n, 8):
                    column = jnp.where(sub == m, w[m][n], column)
                term = column * heads[n][v]
                total = term if total is None else total + term
            rows[b][v] = total
        for g in range(b + 1, groups):
            heads_u = [[sublane(rows[b][v], m) for v in range(vregs)] for m in range(8)]
            for m in range(8):
                coef = w[m][0] * cols[g][0]
                for l in range(1, m + 1):
                    coef = coef + w[m][l] * cols[g][l]
                for v in range(vregs):
                    rows[g][v] = rows[g][v] - coef * heads_u[m][v]
    upper = jnp.concatenate([jnp.concatenate(rows[g], axis=1) for g in range(groups)], axis=0)
    start = pl.multiple_of(p * PANEL, PANEL)
    inv_ref[pl.ds(start, PANEL), :] = upper[:, width:]
    ahead = pltpu.roll(upper[:, :width], width - PANEL, 1)
    h, m, l = split3(jnp.concatenate([ahead, upper[:, width:]], axis=1))
    hg, mg, lg = h[:, :width], m[:, :width], l[:, :width]
    update = tmm(
        jnp.concatenate([hg, hg, mg, mg, hg, lg], axis=0),
        jnp.concatenate([h, m, h, m, l, h], axis=0),
    )
    rest = width - PANEL
    work[0:rest, width:] = work[PANEL:width, width:] - update[:rest, width:]
    work[0:rest, :width] = below - update[:rest, :width]


def inverse_factor(gram, live, work, inv_ref):
    width = gram.shape[0]
    r = lax.broadcasted_iota(jnp.int32, (width, width), 0)
    c = lax.broadcasted_iota(jnp.int32, (width, width), 1)
    eye = jnp.where(r == c, 1.0, 0.0)
    work[:, :width] = gram + eye * (1.0 - live)
    work[:, width:] = eye

    def body(p, carry):
        panel_step(p, work, inv_ref)
        return carry

    lax.fori_loop(0, width // PANEL, body, 0)


def compute_kernel(
    ranks,
    left,
    right,
    probe,
    al,
    ar,
    bl,
    br,
    out_left,
    out_right,
    work,
    inv0,
    inv1,
    s0h,
    s0l,
    s1h,
    s1l,
):
    tile, width = left.shape
    chunks = tile // CHUNK
    crank, t0, t1 = ranks[0], ranks[1], ranks[2]
    lanes = lax.broadcasted_iota(jnp.int32, (1, width), 1)
    subs = lax.broadcasted_iota(jnp.int32, (width, 1), 0)

    def row_mask(count):
        return jnp.where(subs < count, 1.0, 0.0).astype(F32)

    def lane_mask(count):
        return jnp.where(lanes < count, 1.0, 0.0).astype(F32)

    keep = row_mask(crank)
    live0, live1 = lane_mask(t0), lane_mask(t1)
    zero = jnp.zeros((width, width), F32)

    def at(i):
        return pl.ds(pl.multiple_of(i * CHUNK, CHUNK), CHUNK)

    def before(i, carry):
        rp0, rp1 = carry
        rh, rl = split2(right[at(i), :])
        p0, p1 = probe[0, at(i), :], probe[1, at(i), :]
        return rp0 + (tmm(rh, p0) + tmm(rl, p0)), rp1 + (tmm(rh, p1) + tmm(rl, p1))

    core0, rp1 = lax.fori_loop(0, chunks, before, (zero, zero))
    core0 = core0 * keep * live0
    rp1 = rp1 * keep

    def cores(i, carry):
        m0, m1, b00, b01, b11 = carry
        x0, x1 = br[0, at(i), :], br[1, at(i), :]
        p0, p1 = probe[0, at(i), :], probe[1, at(i), :]
        return (
            m0 + tmm(ar[0, at(i), :], bl[0, at(i), :]),
            m1 + tmm(ar[1, at(i), :], bl[1, at(i), :]),
            b00 + tmm(x0, p0),
            b01 + tmm(x0, p1),
            b11 + tmm(x1, p1),
        )

    mid0, mid1, b00, b01, b11 = lax.fori_loop(0, chunks, cores, (zero,) * 5)
    weight0, weight1 = ranks[7].astype(F32), ranks[8].astype(F32)
    mid0 = mid0 * row_mask(ranks[3]) * lane_mask(ranks[5]) * weight0
    mid1 = mid1 * row_mask(ranks[4]) * lane_mask(ranks[6]) * weight1
    sc0 = fine(mm, mid0, b00) * live0
    sc1 = fine(mm, mid1, b11) * live1

    core0h, core0l = split2(core0)
    sc0h, sc0l = split2(sc0)

    def first(i, carry):
        gh, gx, gl, ls, as_ = carry
        lh, ll = split2(left[at(i), :])
        a = al[0, at(i), :]
        s = (mm(lh, core0h) + (mm(lh, core0l) + mm(ll, core0h))) + (mm(a, sc0h) + mm(a, sc0l))
        sh, sl = split2(s)
        s0h[at(i), :] = sh
        s0l[at(i), :] = sl
        return (
            gh + tmm(sh, sh),
            gx + tmm(sh, sl),
            gl + tmm(sl, sl),
            ls + (tmm(lh, sh) + (tmm(lh, sl) + tmm(ll, sh))),
            as_ + (tmm(a, sh) + tmm(a, sl)),
        )

    gh, gx, gl, ls0, as0 = lax.fori_loop(0, chunks, first, (zero,) * 5)
    inverse_factor(gh + (gx + gx.T) + gl, live0, work, inv0)
    w0 = inv0[...]

    y = fine(tmm, ls0, rp1) + fine(tmm, as0, fine(mm, mid0, b01))
    z = fine(tmm, w0, fine(mm, w0, y)) * live1
    zh, zl = split2(z)
    sc1h, sc1l = split2(sc1)

    def second(i, carry):
        gh, gx, gl, ss, as_ = carry
        a = al[1, at(i), :]
        ph, pl_ = s0h[at(i), :], s0l[at(i), :]
        s = (mm(ph, zh) + (mm(ph, zl) + mm(pl_, zh))) + (mm(a, sc1h) + mm(a, sc1l))
        sh, sl = split2(s)
        s1h[at(i), :] = sh
        s1l[at(i), :] = sl
        return (
            gh + tmm(sh, sh),
            gx + tmm(sh, sl),
            gl + tmm(sl, sl),
            ss + (tmm(ph, sh) + (tmm(ph, sl) + tmm(pl_, sh))),
            as_ + (tmm(a, sh) + tmm(a, sl)),
        )

    gh, gx, gl, ss, as1 = lax.fori_loop(0, chunks, second, (zero,) * 5)
    inverse_factor(gh + (gx + gx.T) + gl, live1, work, inv1)
    w1 = inv1[...]

    root = math.sqrt(tile)
    turn = fine(mmt, fine(mm, w0, ss), w1)
    hold = fine(mmt, ls0, w0) * keep
    tr = fine(mm, hold, turn) * (1.0 / root)
    tb0 = fine(tmm, mid0, fine(mm, fine(mmt, as0, w0), turn)) * (1.0 / root)
    tb1 = fine(tmm, mid1, fine(mmt, as1, w1)) * (1.0 / root)
    w1h, w1l = split2(w1 * root)
    trh, trl = split2(tr)
    tb0h, tb0l = split2(tb0)
    tb1h, tb1l = split2(tb1)

    def last(i, carry):
        sh, sl = s1h[at(i), :], s1l[at(i), :]
        out_left[at(i), :] = mmt(sh, w1h) + (mmt(sh, w1l) + mmt(sl, w1h))
        rh, rl = split2(right[at(i), :])
        x0, x1 = br[0, at(i), :], br[1, at(i), :]
        out_right[at(i), :] = (mm(rh, trh) + (mm(rh, trl) + mm(rl, trh))) + (
            (mm(x0, tb0h) + mm(x0, tb0l)) + (mm(x1, tb1h) + mm(x1, tb1l))
        )
        return carry

    lax.fori_loop(0, chunks, last, 0)


def compute(ranks, left, right, probe, al, ar, bl, br):
    tile, width = left.shape
    vmem = pl.BlockSpec(memory_space=pltpu.VMEM)
    return pl.pallas_call(
        compute_kernel,
        out_shape=[jax.ShapeDtypeStruct((tile, width), F32)] * 2,
        in_specs=[pl.BlockSpec(memory_space=pltpu.SMEM)] + [vmem] * 7,
        out_specs=[vmem] * 2,
        scratch_shapes=[
            pltpu.VMEM((width, 2 * width), F32),
            pltpu.VMEM((width, width), F32),
            pltpu.VMEM((width, width), F32),
        ]
        + [pltpu.VMEM((tile, width), BF16)] * 4,
        compiler_params=pltpu.CompilerParams(vmem_limit_bytes=60 * 1024 * 1024),
    )(ranks, left, right, probe, al, ar, bl, br)


class Exchange:
    COPIES = 40

    def __init__(self, k, al_in, ar_in, bl_in, br_in, al, ar, bl, br, send, recv, local):
        self.k = k
        self.send, self.recv, self.local = send, recv, local
        row, col = lax.axis_index("row"), lax.axis_index("col")
        self.x, self.y, self.z = row % 4, (row // 4) % 4, row // 16
        self.h, self.c = col // 2, col % 2
        self.row, self.col = row, col
        self.ins = {"al": al_in, "ar": ar_in, "bl": bl_in, "br": br_in}
        self.full = {"al": al, "ar": ar, "bl": bl, "br": br}
        self.base = k * self.COPIES
        self.offset = {"bl": 0, "br": 11, "ar": 22, "al": 31}

    def at_row(self, x=None, y=None, z=None):
        x = self.x if x is None else x
        y = self.y if y is None else y
        z = self.z if z is None else z
        return ((z * 4 + y) * 4 + x, self.col)

    def at_col(self, h=None, c=None):
        h = self.h if h is None else h
        c = self.c if c is None else c
        return (self.row, h * 2 + c)

    def peers(self):
        yield self.at_row(z=1 - self.z)
        for d in (1, 2, 3):
            yield self.at_row(x=(self.x + d) % 4)
            yield self.at_row(y=(self.y + d) % 4)
        yield self.at_col(h=(self.h + 1) % 4)
        yield self.at_col(h=(self.h + 3) % 4)
        yield self.at_col(c=1 - self.c)

    def copy(self, name, i, src, dst, to):
        n = self.base + self.offset[name] + i
        return pltpu.make_async_remote_copy(
            src_ref=src,
            dst_ref=dst,
            send_sem=self.send.at[n],
            recv_sem=self.recv.at[n],
            device_id=to,
            device_id_type=pl.DeviceIdType.MESH,
        )

    def own(self, name):
        i = ("bl", "br", "ar", "al").index(name)
        src = self.ins[name].at[self.k]
        dst = self.full[name].at[self.k]
        dst = dst.at[self.z, self.y, self.x] if name[0] == "b" else dst.at[self.h, self.c]
        return pltpu.make_async_copy(src, dst, self.local.at[4 * self.k + i])

    def b_pair(self, name):
        src = self.ins[name].at[self.k]
        full = self.full[name].at[self.k]
        return [self.copy(name, 0, src, full.at[self.z, self.y, self.x], self.at_row(z=1 - self.z))]

    def b_near(self, name, second):
        full = self.full[name].at[self.k]
        z = 1 - self.z if second else self.z
        slot = full.at[z, self.y, self.x]
        src = slot if second else self.ins[name].at[self.k]
        out = []
        for d in (1, 2, 3):
            to = self.at_row(x=(self.x + d) % 4) if name == "bl" else self.at_row(y=(self.y + d) % 4)
            out.append(self.copy(name, (3 if second else 0) + d, src, slot, to))
        return out

    def b_line(self, name, place, z=None):
        full = self.full[name].at[self.k]
        if name == "bl":
            return full.at[:, place] if z is None else full.at[z, place]
        return full.at[:, :, place] if z is None else full.at[z, :, place]

    def b_to(self, name, step):
        if name == "bl":
            return self.at_row(y=(self.y + step) % 4)
        return self.at_row(x=(self.x + step) % 4)

    def b_far(self, name):
        here = self.y if name == "bl" else self.x
        line = self.b_line(name, here)
        return [self.copy(name, 7, line, line, self.b_to(name, 1)), self.copy(name, 8, line, line, self.b_to(name, 3))]

    def b_last(self, name):
        here = self.y if name == "bl" else self.x
        back = self.b_line(name, (here + 3) % 4, 0)
        ahead = self.b_line(name, (here + 1) % 4, 1)
        return [self.copy(name, 9, back, back, self.b_to(name, 1)), self.copy(name, 10, ahead, ahead, self.b_to(name, 3))]

    def a_slot(self, name, h, half=None):
        slot = self.full[name].at[self.k].at[h, self.c]
        if half is None:
            return slot
        n = slot.shape[0] // 2
        return slot.at[pl.ds(half * n, n)]

    def a_first(self, name):
        src = self.ins[name].at[self.k]
        slot = self.a_slot(name, self.h)
        return [
            self.copy(name, 0, src, slot, self.at_col(h=(self.h + 1) % 4)),
            self.copy(name, 1, src, slot, self.at_col(h=(self.h + 3) % 4)),
            self.copy(name, 4, src, slot, self.at_col(c=1 - self.c)),
        ]

    def a_second(self, name):
        back = self.a_slot(name, (self.h + 3) % 4, 0)
        ahead = self.a_slot(name, (self.h + 1) % 4, 1)
        return [
            self.copy(name, 2, back, back, self.at_col(h=(self.h + 1) % 4)),
            self.copy(name, 3, ahead, ahead, self.at_col(h=(self.h + 3) % 4)),
        ]

    def a_core(self, name):
        out = []
        for i, d in ((5, 3), (6, 1)):
            slot = self.a_slot(name, (self.h + d) % 4)
            out.append(self.copy(name, i, slot, slot, self.at_col(c=1 - self.c)))
        return out

    def a_core_last(self, name):
        out = []
        for half in (0, 1):
            slot = self.a_slot(name, (self.h + 2) % 4, half)
            out.append(self.copy(name, 7 + half, slot, slot, self.at_col(c=1 - self.c)))
        return out


def start(copies):
    for c in copies:
        c.start()
    return copies


def landed(copies):
    for c in copies:
        c.wait_recv()


def left_here(copies):
    for c in copies:
        c.wait_send()


def greet(exchange):
    barrier = pltpu.get_barrier_semaphore()
    count = 0
    for peer in exchange.peers():
        pl.semaphore_signal(barrier, inc=1, device_id=peer, device_id_type=pl.DeviceIdType.MESH)
        count += 1
    pl.semaphore_wait(barrier, count)


def gather_kernel(al_in, ar_in, bl_in, br_in, al, ar, bl, br, send, recv, local):
    steps = [
        Exchange(k, al_in, ar_in, bl_in, br_in, al, ar, bl, br, send, recv, local) for k in range(2)
    ]
    owns = [e.own(n) for e in steps for n in ("bl", "br", "ar", "al")]
    start(owns)
    greet(steps[0])
    flown = []

    def go(copies):
        flown.extend(copies)
        return start(copies)

    for c in owns:
        c.wait()
    for e in steps:
        pair = {n: go(e.b_pair(n)) for n in ("bl", "br")}
        near = {n: go(e.b_near(n, False)) for n in ("bl", "br")}
        first = {n: go(e.a_first(n)) for n in ("ar", "al")}
        second = {}
        for n in ("bl", "br"):
            landed(pair[n])
            near[n] = near[n] + go(e.b_near(n, True))
        far = {}
        for n in ("bl", "br"):
            landed(near[n])
            far[n] = go(e.b_far(n))
        for n in ("ar", "al"):
            landed(first[n])
            second[n] = go(e.a_second(n))
            first[n] = go(e.a_core(n))
        last = {}
        for n in ("bl", "br"):
            landed(far[n])
            last[n] = go(e.b_last(n))
        for n in ("ar", "al"):
            landed(second[n])
            second[n] = go(e.a_core_last(n))
        for n in ("bl", "br"):
            landed(last[n])
        for n in ("ar", "al"):
            landed(first[n])
            landed(second[n])
    left_here(flown)


def gather(al, ar, bl, br):
    steps, _, width = al.shape
    hbm = pl.BlockSpec(memory_space=pl.ANY)
    a_full = jax.ShapeDtypeStruct((steps, 4, 2, al.shape[1], width), BF16)
    b_full = jax.ShapeDtypeStruct((steps, 2, 4, 4, bl.shape[1], width), BF16)
    out = pl.pallas_call(
        gather_kernel,
        out_shape=[a_full, a_full, b_full, b_full],
        in_specs=[hbm] * 4,
        out_specs=[hbm] * 4,
        scratch_shapes=[
            pltpu.SemaphoreType.DMA((2 * Exchange.COPIES,)),
            pltpu.SemaphoreType.DMA((2 * Exchange.COPIES,)),
            pltpu.SemaphoreType.DMA((8,)),
        ],
        compiler_params=pltpu.CompilerParams(collective_id=0, has_side_effects=True),
    )(al, ar, bl, br)
    return [x.reshape(steps, -1, width) for x in out]


def on_device(c_left, c_right, c_rank, a_left, a_right, a_rank, a_pattern, b_left, b_right, b_rank, b_pattern, probe, target):
    al, ar, bl, br = gather(a_left[0], a_right[0], b_left[:, 0], b_right[:, 0])
    ranks = jnp.concatenate(
        [
            c_rank[0],
            target[0, 0],
            a_rank[0],
            b_rank[:, 0],
            a_pattern[0] * b_pattern[:, 0],
        ]
    )
    left, right = compute(ranks, c_left[0, 0], c_right[0, 0], probe, al, ar, bl, br)
    return left[None, None], right[None, None]


def solution(mesh):
    return jax.shard_map(
        on_device,
        mesh=mesh,
        in_specs=(
            P("row", "col", None, None),
            P("row", "col", None, None),
            P("row", "col"),
            P("row", None, "col", None),
            P("row", None, "col", None),
            P("row", None),
            P("row", None),
            P(None, "col", "row", None),
            P(None, "col", "row", None),
            P(None, "col"),
            P(None, "col"),
            P(),
            P("row", "col", None),
        ),
        out_specs=(P("row", "col", None, None), P("row", "col", None, None)),
        check_vma=False,
    )
```

time: 875 us -> 148 us (0.17); the launches traced: 865 us -> 147 us
  waiting for transfers between devices: 620 us -> 0 us
  Pallas kernels: 0 us -> 144 us
  other arithmetic: 119 us -> 0.68 us
  matrix products: 73.3 us -> 0 us
  local copies, waits for them, and re-layouts: 31.6 us -> 1.28 us
  between operations: 20.7 us -> 1.29 us
    all_gather x8 -> x0, waiting for transfers between devices: 618 us -> none  [the longest x2 261 us: on_device(): lax.all_gather(b_left[step, 0], 'row', axis=0, tiled=True)]
    pallas_call x0 -> x2, Pallas kernels: none -> 144 us  [the longest x1 79.9 us: gather(): pl.pallas_call(gather_kernel, out_shape=[a_full, a_full, b_full, b_full],...]
    another operation x19 -> x0, other arithmetic: 111 us -> none  [the longest x14 69.7 us: recompress(): factor = jnp.linalg.cholesky(gram)]
    dot_general x22 -> x0, matrix products: 60.8 us -> none  [the longest x10 30.3 us: product_of(): jnp.dot(left, right, precision=lax.Precision.HIGHEST, preferred_element_t...]
    slice x9 -> x0, local copies, waits for them, and re-layouts: 13 us -> none  [the longest x2 2.63 us: on_device(): weight = (a_pattern[0, step] * b_pattern[step, 0]).astype(jnp.float32)]
    another operation x10 -> x0, matrix products: 12.5 us -> none  [the longest x6 9.9 us: recompress(): lax.linalg.triangular_solve(factor, sample, left_side=False, lower=True,...]
    unnamed x57 -> x0, local copies, waits for them, and re-layouts: 9.6 us -> none
  transfers between devices with their start and end apart: 8 -> 0, of which waited for: 8 -> 0; matrix products, arithmetic and copies ran while one was open for 14% -> 0% of each run, Pallas kernels for 0% -> 0%
where the time goes in v1:
time: 148 us; the launch traced here: 147 us
  Pallas kernels  144 us (97%)
    pallas_call x1, Pallas kernels, gather(): pl.pallas_call(gather_kernel, out_shape=[a_full, a_full, b_full, b_full],...  79.9 us
    pallas_call x1, Pallas kernels, compute(): pl.pallas_call(compute_kernel, out_shape=[jax.ShapeDtypeStruct((tile, wid...  64.3 us

profile of v1, /device:TPU:1, one launch (start us, length us, event | category | flops | bytes accessed | tf_op | source)
XLA Modules:
  0.0 147.5 jit_solution(1325021779281373759)
XLA Ops:
  1.3 0.7 bitcast_multiply_fusion
  2.0 1.3 concatenate.3.ranks
  3.2 79.9 %shard_map.140 = (bf16[2,4,2,256,256]{4,3,2,1,0:T(8,128)(2,1)}, bf16[2,4,2,256,256]{4,3,2,1,0:T(8,128)(2,1)}, bf16[2,2,4,4,64,256]{5,4,3,2,1,0:T(8,128)(2,1)}, bf16[2,2,4,4,64,256]{5,4,3,2,1,0:T(8,128)(2,1)}) custom-call(bf16[2,256,256]{2,1,0:T(8,128)(2,1)} %bitcast.27, bf16[2,256,256]{2,1,0:T(8,128)(2,1)} %bitcast.28, bf16[2,64,256]{2,1,0:T(8,128)(2,1)} %bitcast.29, ...), custom_call_target="tpu_custom_call" | custom-call | tf_op jit(solution)/shard_map/pallas_call | solution.py:499
  83.2 64.3 %shard_map.141 = (f32[2048,256]{1,0:T(8,128)}, f32[2048,256]{1,0:T(8,128)}) custom-call(s32[9]{0:T(128)} %concatenate.3.ranks, f32[2048,256]{1,0:T(8,128)} %bitcast.21, f32[2048,256]{1,0:T(8,128)} %bitcast.22, bf16[2,2048,256]{2,1,0:T(8,128)(2,1)} %probe.1, bf16[2,2048,256]{2,1,0:T(8,128)(2,1)} %bitcast.23, bf16[2,2048,256]{2,1,0:T(8,128)(2,1)} %bitcast.24, ...), custom_call_target="tpu_custom_call" | custom-call | tf_op jit(solution)/shard_map/pallas_call | solution.py:278

commit v2 on v1

v2 whole, which is shorter than its diff:
```python
import functools
import math

import jax
import jax.numpy as jnp
from jax import lax
from jax.experimental import pallas as pl
from jax.experimental.pallas import tpu as pltpu
from jax.sharding import PartitionSpec as P

F32 = jnp.float32
BF16 = jnp.bfloat16
PANEL = 32
CHUNK = 256
TILE = 2048


def split2(x):
    hi = x.astype(BF16)
    return hi, (x - hi.astype(F32)).astype(BF16)


def split3(x):
    hi = x.astype(BF16)
    rest = x - hi.astype(F32)
    mid = rest.astype(BF16)
    return hi, mid, (rest - mid.astype(F32)).astype(BF16)


def mm(a, b):
    return jnp.dot(a, b, preferred_element_type=F32)


def tmm(a, b):
    return lax.dot_general(a, b, (((0,), (0,)), ((), ())), preferred_element_type=F32)


def mmt(a, b):
    return lax.dot_general(a, b, (((1,), (1,)), ((), ())), preferred_element_type=F32)


def times(op, a, b):
    ah, al = split2(a)
    bh, bl = split2(b)
    return op(ah, bh) + (op(ah, bl) + op(al, bh))


def fine(op, a, b):
    a0, a1, a2 = split3(a)
    b0, b1, b2 = split3(b)
    return op(a0, b0) + ((op(a0, b1) + op(a1, b0)) + (op(a1, b1) + (op(a0, b2) + op(a2, b0))))


def lane(x, c):
    return jnp.broadcast_to(x[:, c : c + 1], (8, 128))


def sublane(x, r):
    return jnp.broadcast_to(x[r : r + 1, :], (8, 128))


def panel_step(p, work, inv_ref, beside):
    width = work.shape[1] // 2
    vregs = work.shape[1] // 128
    groups = PANEL // 8
    rows = [
        [work[8 * g : 8 * g + 8, 128 * v : 128 * v + 128] for v in range(vregs)] for g in range(groups)
    ]
    below = pltpu.roll(work[PANEL:width, :width], width - PANEL, 1)
    sub = lax.broadcasted_iota(jnp.int32, (8, 128), 0)
    beside(p)
    for b in range(groups):
        cols = [[lane(rows[g][0], 8 * b + m) for m in range(8)] for g in range(groups)]
        d = [[sublane(cols[b][n], m) for n in range(m + 1)] for m in range(8)]
        heads = [[sublane(rows[b][v], n) for v in range(vregs)] for n in range(8)]
        w = [[None] * 8 for _ in range(8)]
        low = [[None] * 8 for _ in range(8)]
        for k in range(8):
            r = lax.rsqrt(d[k][k])
            w[k][k] = r
            for m in range(k + 1, 8):
                low[m][k] = d[m][k] * r
            for m in range(k + 1, 8):
                for n in range(k + 1, m + 1):
                    d[m][n] = d[m][n] - low[m][k] * low[n][k]
            for n in range(k):
                total = low[k][n] * w[n][n]
                for l in range(n + 1, k):
                    total = total + low[k][l] * w[l][n]
                w[k][n] = -(total * r)
        for v in range(vregs):
            total = None
            for n in range(8):
                column = jnp.zeros((8, 128), F32)
                for m in range(n, 8):
                    column = jnp.where(sub == m, w[m][n], column)
                term = column * heads[n][v]
                total = term if total is None else total + term
            rows[b][v] = total
        for g in range(b + 1, groups):
            heads_u = [[sublane(rows[b][v], m) for v in range(vregs)] for m in range(8)]
            for m in range(8):
                coef = w[m][0] * cols[g][0]
                for l in range(1, m + 1):
                    coef = coef + w[m][l] * cols[g][l]
                for v in range(vregs):
                    rows[g][v] = rows[g][v] - coef * heads_u[m][v]
    upper = jnp.concatenate([jnp.concatenate(rows[g], axis=1) for g in range(groups)], axis=0)
    start = pl.multiple_of(p * PANEL, PANEL)
    inv_ref[pl.ds(start, PANEL), :] = upper[:, width:]
    ahead = pltpu.roll(upper[:, :width], width - PANEL, 1)
    h, m, l = split3(jnp.concatenate([ahead, upper[:, width:]], axis=1))
    hg, mg, lg = h[:, :width], m[:, :width], l[:, :width]
    update = tmm(
        jnp.concatenate([hg, hg, mg, mg, hg, lg], axis=0),
        jnp.concatenate([h, m, h, m, l, h], axis=0),
    )
    rest = width - PANEL
    work[0:rest, width:] = work[PANEL:width, width:] - update[:rest, width:]
    work[0:rest, :width] = below - update[:rest, :width]


def inverse_factor(gram, live, work, inv_ref, between, beside):
    width = gram.shape[0]
    r = lax.broadcasted_iota(jnp.int32, (width, width), 0)
    c = lax.broadcasted_iota(jnp.int32, (width, width), 1)
    eye = jnp.where(r == c, 1.0, 0.0)
    work[:, :width] = gram + eye * (1.0 - live)
    work[:, width:] = eye

    def body(p, carry):
        between(p)
        panel_step(p, work, inv_ref, beside)
        return carry

    lax.fori_loop(0, width // PANEL, body, 0)


class Exchange:
    COPIES = 40

    def __init__(self, k, al_in, ar_in, bl_in, br_in, al, ar, bl, br, send, recv, local):
        self.k = k
        self.send, self.recv, self.local = send, recv, local
        row, col = lax.axis_index("row"), lax.axis_index("col")
        self.x, self.y, self.z = row % 4, (row // 4) % 4, row // 16
        self.h, self.c = col // 2, col % 2
        self.row, self.col = row, col
        self.ins = {"al": al_in, "ar": ar_in, "bl": bl_in, "br": br_in}
        self.full = {"al": al, "ar": ar, "bl": bl, "br": br}
        self.base = k * self.COPIES
        self.offset = {"bl": 0, "br": 11, "ar": 22, "al": 31}

    def at_row(self, x=None, y=None, z=None):
        x = self.x if x is None else x
        y = self.y if y is None else y
        z = self.z if z is None else z
        return ((z * 4 + y) * 4 + x, self.col)

    def at_col(self, h=None, c=None):
        h = self.h if h is None else h
        c = self.c if c is None else c
        return (self.row, h * 2 + c)

    def peers(self):
        yield self.at_row(z=1 - self.z)
        for d in (1, 2, 3):
            yield self.at_row(x=(self.x + d) % 4)
            yield self.at_row(y=(self.y + d) % 4)
        yield self.at_col(h=(self.h + 1) % 4)
        yield self.at_col(h=(self.h + 3) % 4)
        yield self.at_col(c=1 - self.c)

    def copy(self, name, i, src, dst, to):
        n = self.base + self.offset[name] + i
        return pltpu.make_async_remote_copy(
            src_ref=src,
            dst_ref=dst,
            send_sem=self.send.at[n],
            recv_sem=self.recv.at[n],
            device_id=to,
            device_id_type=pl.DeviceIdType.MESH,
        )

    def own(self, name):
        i = ("bl", "br", "ar", "al").index(name)
        src = self.ins[name].at[self.k]
        dst = self.full[name].at[self.k]
        dst = dst.at[self.z, self.y, self.x] if name[0] == "b" else dst.at[self.h, self.c]
        return pltpu.make_async_copy(src, dst, self.local.at[4 * self.k + i])

    def b_pair(self, name):
        src = self.ins[name].at[self.k]
        full = self.full[name].at[self.k]
        return [self.copy(name, 0, src, full.at[self.z, self.y, self.x], self.at_row(z=1 - self.z))]

    def b_near(self, name, second):
        full = self.full[name].at[self.k]
        z = 1 - self.z if second else self.z
        slot = full.at[z, self.y, self.x]
        src = slot if second else self.ins[name].at[self.k]
        out = []
        for d in (1, 2, 3):
            to = self.at_row(x=(self.x + d) % 4) if name == "bl" else self.at_row(y=(self.y + d) % 4)
            out.append(self.copy(name, (3 if second else 0) + d, src, slot, to))
        return out

    def b_line(self, name, place, z=None):
        full = self.full[name].at[self.k]
        if name == "bl":
            return full.at[:, place] if z is None else full.at[z, place]
        return full.at[:, :, place] if z is None else full.at[z, :, place]

    def b_to(self, name, step):
        if name == "bl":
            return self.at_row(y=(self.y + step) % 4)
        return self.at_row(x=(self.x + step) % 4)

    def b_far(self, name):
        here = self.y if name == "bl" else self.x
        line = self.b_line(name, here)
        return [self.copy(name, 7, line, line, self.b_to(name, 1)), self.copy(name, 8, line, line, self.b_to(name, 3))]

    def b_last(self, name):
        here = self.y if name == "bl" else self.x
        back = self.b_line(name, (here + 3) % 4, 0)
        ahead = self.b_line(name, (here + 1) % 4, 1)
        return [self.copy(name, 9, back, back, self.b_to(name, 1)), self.copy(name, 10, ahead, ahead, self.b_to(name, 3))]

    def a_slot(self, name, h, half=None):
        slot = self.full[name].at[self.k].at[h, self.c]
        if half is None:
            return slot
        n = slot.shape[0] // 2
        return slot.at[pl.ds(half * n, n)]

    def a_first(self, name):
        src = self.ins[name].at[self.k]
        slot = self.a_slot(name, self.h)
        return [
            self.copy(name, 0, src, slot, self.at_col(h=(self.h + 1) % 4)),
            self.copy(name, 1, src, slot, self.at_col(h=(self.h + 3) % 4)),
            self.copy(name, 4, src, slot, self.at_col(c=1 - self.c)),
        ]

    def a_second(self, name):
        back = self.a_slot(name, (self.h + 3) % 4, 0)
        ahead = self.a_slot(name, (self.h + 1) % 4, 1)
        return [
            self.copy(name, 2, back, back, self.at_col(h=(self.h + 1) % 4)),
            self.copy(name, 3, ahead, ahead, self.at_col(h=(self.h + 3) % 4)),
        ]

    def a_core(self, name):
        out = []
        for i, d in ((5, 3), (6, 1)):
            slot = self.a_slot(name, (self.h + d) % 4)
            out.append(self.copy(name, i, slot, slot, self.at_col(c=1 - self.c)))
        return out

    def a_core_last(self, name):
        out = []
        for half in (0, 1):
            slot = self.a_slot(name, (self.h + 2) % 4, half)
            out.append(self.copy(name, 7 + half, slot, slot, self.at_col(c=1 - self.c)))
        return out


def start(copies):
    for c in copies:
        c.start()
    return copies


def landed(copies):
    for c in copies:
        c.wait_recv()


def left_here(copies):
    for c in copies:
        c.wait_send()


def greet(exchange):
    barrier = pltpu.get_barrier_semaphore()
    count = 0
    for peer in exchange.peers():
        pl.semaphore_signal(barrier, inc=1, device_id=peer, device_id_type=pl.DeviceIdType.MESH)
        count += 1
    pl.semaphore_wait(barrier, count)


def tile_kernel(
    c_rank,
    target,
    a_rank,
    a_pattern,
    b_rank,
    b_pattern,
    left_in,
    right_in,
    probe_in,
    al_in,
    ar_in,
    bl_in,
    br_in,
    s1h_out,
    s1l_out,
    rr_out,
    w1_out,
    left,
    right,
    probe,
    al,
    ar,
    bl,
    br,
    part,
    rr,
    s0h,
    s0l,
    s1h,
    s1l,
    work,
    inv0,
    inv1,
    ls0_ref,
    as0_ref,
    send,
    recv,
    local,
    io,
):
    tile, width = left.shape
    chunks = tile // CHUNK
    loads = [
        pltpu.make_async_copy(right_in, right, io.at[0]),
        pltpu.make_async_copy(probe_in, probe, io.at[1]),
        pltpu.make_async_copy(left_in, left, io.at[2]),
    ]
    start(loads)
    e0, e1 = [Exchange(k, al_in, ar_in, bl_in, br_in, al, ar, bl, br, send, recv, local) for k in range(2)]
    owns = [e.own(n) for e in (e0, e1) for n in ("bl", "br", "ar", "al")]
    start(owns)
    greet(e0)

    lanes = lax.broadcasted_iota(jnp.int32, (1, width), 1)
    subs = lax.broadcasted_iota(jnp.int32, (width, 1), 0)

    def row_mask(count):
        return jnp.where(subs < count, 1.0, 0.0).astype(F32)

    def lane_mask(count):
        return jnp.where(lanes < count, 1.0, 0.0).astype(F32)

    keep = row_mask(c_rank[0, 0])
    live0, live1 = lane_mask(target[0, 0]), lane_mask(target[0, 1])
    zero = jnp.zeros((width, width), F32)

    def at(i):
        return pl.ds(pl.multiple_of(i * CHUNK, CHUNK), CHUNK)

    def a_chunk(ref, k, i):
        return ref[k, i // 2, i % 2]

    def b_chunk(ref, k, i):
        return ref[k, i // 4, i % 4].reshape(CHUNK, width)

    def send_first(e):
        for n in ("bl", "br"):
            start(e.b_pair(n))
        for n in ("bl", "br"):
            start(e.b_near(n, False))
        for n in ("ar", "al"):
            start(e.a_first(n))

    def send_near(e):
        for n in ("bl", "br"):
            landed(e.b_pair(n))
            start(e.b_near(n, True))

    def send_far(e):
        for n in ("bl", "br"):
            landed(e.b_near(n, False))
            landed(e.b_near(n, True))
            start(e.b_far(n))

    def send_last(e):
        for n in ("bl", "br"):
            landed(e.b_far(n))
            start(e.b_last(n))

    def send_second(e, n):
        landed(e.a_first(n))
        start(e.a_second(n))
        start(e.a_core(n))

    def send_core(e, n):
        landed(e.a_second(n))
        start(e.a_core_last(n))

    def have_b(e):
        for n in ("bl", "br"):
            landed(e.b_last(n))

    def have_a(e, n):
        landed(e.a_core(n))
        landed(e.a_core_last(n))

    for c in owns:
        c.wait()
    send_first(e0)
    loads[0].wait()
    loads[1].wait()

    def before(i, carry):
        rp0, rp1 = carry
        rh, rl = split2(right[at(i), :])
        p0, p1 = probe[0, at(i), :], probe[1, at(i), :]
        return rp0 + (tmm(rh, p0) + tmm(rl, p0)), rp1 + (tmm(rh, p1) + tmm(rl, p1))

    rps = lax.fori_loop(0, 3, before, (zero, zero))
    send_near(e0)
    core0, rp1 = lax.fori_loop(3, chunks, before, rps)
    core0 = core0 * keep * live0
    rp1 = rp1 * keep
    core0h, core0l = split2(core0)
    send_far(e0)
    send_second(e0, "ar")
    loads[2].wait()

    def partly(i, carry):
        lh, ll = split2(left[at(i), :])
        part[at(i), :] = mm(lh, core0h) + (mm(lh, core0l) + mm(ll, core0h))
        return carry

    lax.fori_loop(0, chunks, partly, 0)
    send_second(e0, "al")
    send_last(e0)
    send_first(e1)
    send_core(e0, "ar")
    have_b(e0)

    def probed(i, carry):
        b00, b01 = carry
        x0 = b_chunk(br, 0, i)
        return b00 + tmm(x0, probe[0, at(i), :]), b01 + tmm(x0, probe[1, at(i), :])

    b00, b01 = lax.fori_loop(0, chunks, probed, (zero, zero))
    have_a(e0, "ar")

    def middles(i, total):
        return total + tmm(a_chunk(ar, 0, i), b_chunk(bl, 0, i))

    mid0 = lax.fori_loop(0, chunks, middles, zero)
    weight0 = (a_pattern[0, 0] * b_pattern[0, 0]).astype(F32)
    weight1 = (a_pattern[0, 1] * b_pattern[1, 0]).astype(F32)
    mid0 = mid0 * row_mask(a_rank[0, 0]) * lane_mask(b_rank[0, 0]) * weight0
    sc0 = fine(mm, mid0, b00) * live0
    mb0 = fine(mm, mid0, b01)
    sc0h, sc0l = split2(sc0)
    send_near(e1)
    send_core(e0, "al")
    have_a(e0, "al")

    def first(i, carry):
        gh, gx, gl = carry
        a = a_chunk(al, 0, i)
        s = part[at(i), :] + (mm(a, sc0h) + mm(a, sc0l))
        sh, sl = split2(s)
        s0h[at(i), :] = sh
        s0l[at(i), :] = sl
        return gh + tmm(sh, sh), gx + tmm(sh, sl), gl + tmm(sl, sl)

    gh, gx, gl = lax.fori_loop(0, chunks, first, (zero,) * 3)
    ls0_ref[...] = zero
    as0_ref[...] = zero
    send_far(e1)
    send_second(e1, "ar")

    def between0(p):
        @pl.when(p == 1)
        def _():
            send_second(e1, "al")

        @pl.when(p == 2)
        def _():
            send_last(e1)
            send_core(e1, "ar")

        @pl.when(p == 4)
        def _():
            send_core(e1, "al")

    def beside0(p):
        lh, ll = split2(left[at(p), :])
        sh, sl = s0h[at(p), :], s0l[at(p), :]
        a = a_chunk(al, 0, p)
        ls0_ref[...] += tmm(lh, sh) + (tmm(lh, sl) + tmm(ll, sh))
        as0_ref[...] += tmm(a, sh) + tmm(a, sl)

    inverse_factor(gh + (gx + gx.T) + gl, live0, work, inv0, between0, beside0)
    w0, ls0, as0 = inv0[...], ls0_ref[...], as0_ref[...]
    have_b(e1)
    have_a(e1, "ar")
    have_a(e1, "al")

    def cores(i, carry):
        mid, b11 = carry
        return (
            mid + tmm(a_chunk(ar, 1, i), b_chunk(bl, 1, i)),
            b11 + tmm(b_chunk(br, 1, i), probe[1, at(i), :]),
        )

    mid1, b11 = lax.fori_loop(0, chunks, cores, (zero, zero))
    mid1 = mid1 * row_mask(a_rank[0, 1]) * lane_mask(b_rank[1, 0]) * weight1
    sc1 = fine(mm, mid1, b11) * live1
    y = fine(tmm, ls0, rp1) + fine(tmm, as0, mb0)
    z = fine(tmm, w0, fine(mm, w0, y)) * live1
    zh, zl = split2(z)
    sc1h, sc1l = split2(sc1)

    def second(i, carry):
        gh, gx, gl, ss, as_ = carry
        a = a_chunk(al, 1, i)
        ph, pl_ = s0h[at(i), :], s0l[at(i), :]
        s = (mm(ph, zh) + (mm(ph, zl) + mm(pl_, zh))) + (mm(a, sc1h) + mm(a, sc1l))
        sh, sl = split2(s)
        s1h[at(i), :] = sh
        s1l[at(i), :] = sl
        return (
            gh + tmm(sh, sh),
            gx + tmm(sh, sl),
            gl + tmm(sl, sl),
            ss + (tmm(ph, sh) + (tmm(ph, sl) + tmm(pl_, sh))),
            as_ + (tmm(a, sh) + tmm(a, sl)),
        )

    gh, gx, gl, ss, as1 = lax.fori_loop(0, chunks, second, (zero,) * 5)
    stores = [
        pltpu.make_async_copy(s1h, s1h_out, io.at[0]),
        pltpu.make_async_copy(s1l, s1l_out, io.at[1]),
        pltpu.make_async_copy(rr, rr_out, io.at[2]),
    ]
    start(stores[:2])
    turn = fine(mm, w0, ss)
    tr = fine(mm, fine(mmt, ls0, w0) * keep, turn)
    tb0 = fine(tmm, mid0, fine(mm, fine(mmt, as0, w0), turn))
    tb1 = fine(tmm, mid1, as1)
    trh, trl = split2(tr)
    tb0h, tb0l = split2(tb0)
    tb1h, tb1l = split2(tb1)

    def beside1(p):
        rh, rl = split2(right[at(p), :])
        x0, x1 = b_chunk(br, 0, p), b_chunk(br, 1, p)
        rr[at(p), :] = (mm(rh, trh) + (mm(rh, trl) + mm(rl, trh))) + (
            (mm(x0, tb0h) + mm(x0, tb0l)) + (mm(x1, tb1h) + mm(x1, tb1l))
        )

    inverse_factor(gh + (gx + gx.T) + gl, live1, work, inv1, lambda p: None, beside1)
    start(stores[2:])
    w1_out[...] = inv1[...]
    for e in (e0, e1):
        for n in ("bl", "br"):
            for copies in (e.b_pair(n), e.b_near(n, False), e.b_near(n, True), e.b_far(n), e.b_last(n)):
                left_here(copies)
        for n in ("ar", "al"):
            for copies in (e.a_first(n), e.a_second(n), e.a_core(n), e.a_core_last(n)):
                left_here(copies)
    for c in stores:
        c.wait()


def update(c_rank, target, a_rank, a_pattern, b_rank, b_pattern, left, right, probe, al, ar, bl, br):
    tile, width = left.shape
    steps = probe.shape[0]
    rows = al.shape[1]
    vmem = pl.BlockSpec(memory_space=pltpu.VMEM)
    smem = pl.BlockSpec(memory_space=pltpu.SMEM)
    hbm = pl.BlockSpec(memory_space=pl.ANY)
    a_full = pltpu.VMEM((steps, 4, 2, rows, width), BF16)
    b_full = pltpu.VMEM((steps, 2, 4, 4, bl.shape[1], width), BF16)
    square = pltpu.VMEM((width, width), F32)
    return pl.pallas_call(
        tile_kernel,
        out_shape=[
            jax.ShapeDtypeStruct((tile, width), BF16),
            jax.ShapeDtypeStruct((tile, width), BF16),
            jax.ShapeDtypeStruct((tile, width), F32),
            jax.ShapeDtypeStruct((width, width), F32),
        ],
        in_specs=[smem] * 6 + [hbm] * 3 + [vmem] * 4,
        out_specs=[hbm] * 3 + [vmem],
        scratch_shapes=[
            pltpu.VMEM((tile, width), F32),
            pltpu.VMEM((tile, width), F32),
            pltpu.VMEM((steps, tile, width), BF16),
            a_full,
            a_full,
            b_full,
            b_full,
            pltpu.VMEM((tile, width), F32),
            pltpu.VMEM((tile, width), F32),
        ]
        + [pltpu.VMEM((tile, width), BF16)] * 4
        + [pltpu.VMEM((width, 2 * width), F32)]
        + [square] * 4
        + [
            pltpu.SemaphoreType.DMA((2 * Exchange.COPIES,)),
            pltpu.SemaphoreType.DMA((2 * Exchange.COPIES,)),
            pltpu.SemaphoreType.DMA((8,)),
            pltpu.SemaphoreType.DMA((3,)),
        ],
        compiler_params=pltpu.CompilerParams(
            collective_id=0, has_side_effects=True, vmem_limit_bytes=60 * 1024 * 1024
        ),
    )(c_rank, target, a_rank, a_pattern, b_rank, b_pattern, left, right, probe, al, ar, bl, br)


def finish_kernel(w1, sh, sl, rr, out_left, out_right, wh, wl):
    root = math.sqrt(TILE)

    @pl.when(pl.program_id(0) == 0)
    def _():
        h, l = split2(w1[...])
        wh[...] = h
        wl[...] = l

    h, l = wh[...], wl[...]
    out_left[...] = (mmt(sh[...], h) + (mmt(sh[...], l) + mmt(sl[...], h))) * root
    rh, rl = split2(rr[...])
    out_right[...] = (mmt(rh, h) + (mmt(rh, l) + mmt(rl, h))) * (1.0 / root)


def finish(w1, sh, sl, rr):
    tile, width = rr.shape
    block = pl.BlockSpec((CHUNK, width), lambda i: (i, 0))
    return pl.pallas_call(
        finish_kernel,
        grid=(tile // CHUNK,),
        out_shape=[jax.ShapeDtypeStruct((tile, width), F32)] * 2,
        in_specs=[pl.BlockSpec((width, width), lambda i: (0, 0)), block, block, block],
        out_specs=[block, block],
        scratch_shapes=[pltpu.VMEM((width, width), BF16)] * 2,
    )(w1, sh, sl, rr)


def on_device(c_left, c_right, c_rank, a_left, a_right, a_rank, a_pattern, b_left, b_right, b_rank, b_pattern, probe, target):
    sh, sl, rr, w1 = update(
        c_rank,
        target[0],
        a_rank,
        a_pattern,
        b_rank,
        b_pattern,
        c_left[0, 0],
        c_right[0, 0],
        probe,
        a_left[0],
        a_right[0],
        b_left[:, 0],
        b_right[:, 0],
    )
    left, right = finish(w1, sh, sl, rr)
    return left[None, None], right[None, None]


def solution(mesh):
    return jax.shard_map(
        on_device,
        mesh=mesh,
        in_specs=(
            P("row", "col", None, None),
            P("row", "col", None, None),
            P("row", "col"),
            P("row", None, "col", None),
            P("row", None, "col", None),
            P("row", None),
            P("row", None),
            P(None, "col", "row", None),
            P(None, "col", "row", None),
            P(None, "col"),
            P(None, "col"),
            P(),
            P("row", "col", None),
        ),
        out_specs=(P("row", "col", None, None), P("row", "col", None, None)),
        check_vma=False,
    )
```

time: 148 us -> 108 us (0.73)
  Pallas kernels: 144 us -> 104 us
    pallas_call x2, Pallas kernels: 144 us -> 104 us  [the longest x1 95.8 us: update(): pl.pallas_call(tile_kernel, out_shape=[jax.ShapeDtypeStruct((tile, width)...]
    unnamed x0 -> x2, local copies, waits for them, and re-layouts: none -> 2.59 us
where the time goes in v2:
time: 108 us
  Pallas kernels  104 us (96%)
  local copies, waits for them, and re-layouts  2.59 us (2%)
  between operations  1.29 us (1%)
    pallas_call x1, Pallas kernels, update(): pl.pallas_call(tile_kernel, out_shape=[jax.ShapeDtypeStruct((tile, width)...  95.8 us
    pallas_call x1, Pallas kernels, finish(): pl.pallas_call(finish_kernel, grid=(tile // CHUNK,), out_shape=[jax.Shape...  8.08 us
    unnamed x2, local copies, waits for them, and re-layouts  2.59 us

profile of v2, /device:TPU:1, one launch (start us, length us, event | category | flops | bytes accessed | tf_op | source)
XLA Modules:
  0.0 107.8 jit_solution(17340244023947418392)
XLA Ops:
  1.3 1.3 %copy.15.b_rank = s32[2,1]{1,0:T(2,128)} copy(s32[2,1]{0,1:T(1,128)} %param.22) | data formatting | bytes 16 | tf_op args[9]
  2.6 1.3 %copy.16.b_pattern = s32[2,1]{1,0:T(2,128)} copy(s32[2,1]{0,1:T(1,128)} %param.23) | data formatting | bytes 16 | tf_op args[10]
  3.9 95.8 %shard_map.140 = (bf16[2048,256]{1,0:T(8,128)(2,1)}, bf16[2048,256]{1,0:T(8,128)(2,1)}, f32[2048,256]{1,0:T(8,128)}, f32[256,256]{1,0:T(8,128)}) custom-call(s32[1,1]{1,0:T(1,128)S(6)} %copy.17.c_rank, s32[1,2]{1,0:T(1,128)} %bitcast.15, s32[1,2]{1,0:T(1,128)} %a_rank.1, s32[1,2]{1,0:T(1,128)} %a_pattern.1, s32[2,1]{1,0:T(2,128)} %copy.15.b_rank, ...), custom_call_target="tpu_custom_call" | custom-call | tf_op jit(solution)/shard_map/pallas_call | solution.py:586
  99.7 8.1 %shard_map.141 = (f32[2048,256]{1,0:T(8,128)}, f32[2048,256]{1,0:T(8,128)}) custom-call(f32[256,256]{1,0:T(8,128)} %get-tuple-element.8.w1, bf16[2048,256]{1,0:T(8,128)(2,1)} %get-tuple-element.9.sh, bf16[2048,256]{1,0:T(8,128)(2,1)} %get-tuple-element.10.sl, f32[2048,256]{1,0:T(8,128)} %get-tuple-element.11.rr), custom_call_target="tpu_custom_call" | custom-call | tf_op jit(solution)/shard_map/pallas_call | solution.py:640
